TPU v7x, 32 devices: a whole 2x2x4 slice. The times are simulated.
32 devices in a mesh: outer: 4 (over y, core), inner: 8 (over z, x).
Axes of the slice: x: 2, y: 2, z: 4, core: 2. Of those that a mesh axis runs over, the one named last changes fastest.
Arguments:
- queries: bfloat16 [8192, 1024], P(('outer', 'inner')), may hold values from -100 to 100
- keys: bfloat16 [8192, 1024], P(('outer', 'inner')), may hold values from -6 to 6
- values: bfloat16 [8192, 1024], P(('outer', 'inner')), may hold values from -6 to 6
- modality: int32 [8192], P(('outer', 'inner')), may hold values 0 or 1
Outputs:
- attended: bfloat16 [8192, 1024], P(('outer', 'inner'))
All inputs are finite; a program needn't handle non-finite values. No bound on the sum of `modality` on one device may be relied on, other than what follows from the above.
Results may differ from a plain program's by a relative error of at most 0.0034.
Values may be sent and summed in bfloat16 or wider, within the bound.
A program may use at most 128 MiB of HBM per device.

v0:
```python
import jax
import jax.numpy as jnp
from jax import lax
from jax.sharding import PartitionSpec as P

HEAD_DIM = 128
BLOCK = 128


def padded_2(cells, sides, width):
    for axis, dim in sides:
        count = lax.axis_size(axis)
        ends = count - 1
        head = lax.slice_in_dim(cells, 0, width, axis=dim)
        tail = lax.slice_in_dim(cells, cells.shape[dim] - width, cells.shape[dim], axis=dim)
        cells = jnp.concatenate(
            [
                lax.ppermute(tail, axis, [(i, (i + 1) % count) for i in range(ends)]),
                cells,
                lax.ppermute(head, axis, [((i + 1) % count, i) for i in range(ends)]),
            ],
            axis=dim,
        )
    return cells


def partner_2(block, axis, stride):
    count = lax.axis_size(axis)
    route = []
    for low in range(count):
        high = low | 1 << stride
        if high != low and high < count:
            route += [(low, high), (high, low)]
    return lax.ppermute(block, axis, route)


def coarsen(stacked):
    paired = stacked.astype(jnp.float32).reshape(
        stacked.shape[0], stacked.shape[1] // 2, 2, stacked.shape[2]
    )
    return (0.5 * (paired[:, :, 0] + paired[:, :, 1])).astype(jnp.bfloat16)


def ordered(own_node, partner, upper_half):
    first_node = jnp.where(upper_half == 0, own_node, partner)
    second = jnp.where(upper_half == 0, partner, own_node)
    return coarsen(jnp.concatenate([first_node, second], axis=1))


def attend(query_rows, groups):
    total_rows, row_width = query_rows.shape
    head_count = row_width // HEAD_DIM
    score_scale = HEAD_DIM ** (-0.5)
    per_head = query_rows.reshape(total_rows, head_count, HEAD_DIM)
    scores = []
    row_best = None
    for stacked, allowed in groups:
        group_count = stacked.shape[1]
        key_span = stacked.shape[2]
        grouped = per_head.reshape(group_count, total_rows // group_count, head_count, HEAD_DIM)
        key_heads = stacked[0].reshape(group_count, key_span, head_count, HEAD_DIM)
        logits = (
            jnp.einsum("gqhd,gkhd->ghqk", grouped, key_heads, preferred_element_type=jnp.float32)
            * score_scale
        )
        if allowed is not None:
            logits = jnp.where(allowed[:, None], logits, -jnp.inf)
        row_peak = jnp.max(logits, axis=3).transpose(1, 0, 2).reshape(head_count, total_rows)
        row_best = row_peak if row_best is None else jnp.maximum(row_best, row_peak)
        scores.append(logits)
    denominator = jnp.zeros((head_count, total_rows), jnp.float32)
    numerator = jnp.zeros((total_rows, head_count, HEAD_DIM), jnp.float32)
    for logits, (stacked, allowed) in zip(scores, groups):
        group_count = stacked.shape[1]
        key_span = stacked.shape[2]
        row_shift = row_best.reshape(head_count, group_count, total_rows // group_count).transpose(
            1, 0, 2
        )
        weights = jnp.exp(logits - row_shift[:, :, :, None])
        denominator = denominator + jnp.sum(weights, axis=3).transpose(1, 0, 2).reshape(
            head_count, total_rows
        )
        value_heads = stacked[1].reshape(group_count, key_span, head_count, HEAD_DIM)
        mixture = jnp.einsum(
            "ghqk,gkhd->gqhd",
            weights.astype(jnp.bfloat16),
            value_heads,
            preferred_element_type=jnp.float32,
        )
        numerator = numerator + mixture.reshape(total_rows, head_count, HEAD_DIM)
    result = numerator / denominator.T[:, :, None]
    return result.reshape(total_rows, row_width).astype(jnp.bfloat16)


def shards(queries, keys, values, modality):
    tok_rows, row_width = queries.shape
    block_count = tok_rows // BLOCK
    device_count = lax.axis_size(("outer", "inner"))
    device_index = lax.axis_index(("outer", "inner"))
    stacked = jnp.stack([keys, values])
    labels = modality.astype(jnp.bfloat16)[None, :]
    padded, padded_labels = (
        padded_2(stacked, ((("outer", "inner"), 1),), BLOCK),
        padded_2(labels, ((("outer", "inner"), 1),), BLOCK),
    )
    positions = jnp.arange(tok_rows + 2 * BLOCK)
    outside = (positions < BLOCK) & (device_index == 0) | (positions >= tok_rows + BLOCK) & (
        device_index == device_count - 1
    )
    key_labels = jnp.where(outside, -1.0, padded_labels[0].astype(jnp.float32))
    query_labels = modality.astype(jnp.float32).reshape(block_count, BLOCK)
    near_prev = padded[:, :tok_rows].reshape(2, block_count, BLOCK, row_width)
    near_here = padded[:, BLOCK : tok_rows + BLOCK].reshape(2, block_count, BLOCK, row_width)
    near_next = padded[:, 2 * BLOCK :].reshape(2, block_count, BLOCK, row_width)
    near_kv = jnp.concatenate([near_prev, near_here, near_next], axis=2)
    label_rows = jnp.concatenate(
        [
            key_labels[:tok_rows].reshape(block_count, BLOCK),
            key_labels[BLOCK : tok_rows + BLOCK].reshape(block_count, BLOCK),
            key_labels[2 * BLOCK :].reshape(block_count, BLOCK),
        ],
        axis=1,
    )
    columns = jnp.arange(3 * BLOCK)
    middle = (columns >= BLOCK) & (columns < 2 * BLOCK)
    near_mask = (label_rows[:, None, :] == query_labels[:, :, None]) | middle[None, None, :]
    own_node = coarsen(stacked)
    far_sets = []
    for bit_index in range(device_count.bit_length() - 1):
        partner = partner_2(own_node, ("outer", "inner"), bit_index)
        far_sets.append(partner)
        own_node = ordered(own_node, partner, device_index // 2**bit_index % 2)
    half_rows = tok_rows // 2
    half_blocks = block_count // 2
    outputs = []
    for half_index in range(2):
        lower = half_index * half_blocks
        groups = [(near_kv[:, lower : lower + half_blocks], near_mask[lower : lower + half_blocks])]
        for partner in far_sets:
            groups.append((partner[:, None], None))
        outputs.append(
            attend(queries[half_index * half_rows : (half_index + 1) * half_rows], groups)
        )
    return jnp.concatenate(outputs, axis=0)


def solution(mesh):
    placed = (
        P(("outer", "inner"), None),
        P(("outer", "inner"), None),
        P(("outer", "inner"), None),
        P(("outer", "inner")),
    )
    return jax.shard_map(
        shards, mesh=mesh, in_specs=placed, out_specs=P(("outer", "inner"), None), check_vma=False
    )
```

profile of v0, /device:TPU:0, one launch (start us, length us, event | category | flops | bytes accessed | tf_op | source)
XLA Modules:
  0.0 168.9 jit_solution(16045545202861996716)
XLA Ops:
  0.0 1.2 stack.27
  1.2 1.2 stack.28
  2.5 1.3 maximum_convert_fusion
  3.9 1.5 fusion.29
  6.4 3.0 %collective-permute-start.4 = (bf16[2,128,1024]{2,1,0:T(8,128)(2,1)}, bf16[2,128,1024]{2,1,0:T(8,128)(2,1)S(1)}, u32[]{:S(2)}, u32[]{:S(2)}) collective-permute-start(bf16[2,128,1024]{2,1,0:T(8,128)(2,1)} %bitcast.139), channel_id=1, source_target_pairs={{0,1},{1,0},{2,3},{3,2},{4,5},{5,4},{6,7},{7,6},{8,9},{9,8},{10,11... | collective-permute-start | bytes 1572872 | tf_op jit(solution)/shard_map/ppermute | solution.py:34
  9.4 1.9 %collective-permute-start.2 = (bf16[1,128]{1,0:T(2,128)(2,1)S(1)}, bf16[1,128]{1,0:T(2,128)(2,1)S(1)}, u32[]{:S(2)}, u32[]{:S(2)}) collective-permute-start(bf16[1,128]{1,0:T(2,128)(2,1)S(1)} %get-tuple-element.56), channel_id=1, source_target_pairs={{0,1},{1,2},{2,3},{3,4},{4,5},{5,6},{6,7},{7,8},{8,9},{9,10},{10,1... | collective-permute-start | bytes 776 | tf_op jit(solution)/shard_map/ppermute | solution.py:18
  11.3 1.3 collective-permute-start.3
  13.7 6.4 %collective-permute-start = (bf16[2,128,1024]{2,1,0:T(8,128)(2,1)}, bf16[2,128,1024]{2,1,0:T(8,128)(2,1)}, u32[]{:S(2)}, u32[]{:S(2)}) collective-permute-start(bf16[2,128,1024]{2,1,0:T(8,128)(2,1)} %get-tuple-element.29), channel_id=1, source_target_pairs={{0,1},{1,2},{2,3},{3,4},{4,5},{5,6},{6,7},{7,8},{8,9},{9,10},{10,1... | collective-permute-start | bytes 1572872 | tf_op jit(solution)/shard_map/ppermute | solution.py:18
  20.0 1.3 collective-permute-start.1
  24.0 1.6 copy.219
  26.4 2.3 %fusion.25 = bf16[2,128,1,1024]{3,2,1,0:T(2,128)(2,1)S(1)} fusion(f32[2,128,1,1024]{3,0,2,1:T(2,128)S(1)} %get-tuple-element.26, f32[2,128,1,1024]{3,0,2,1:T(2,128)S(1)} %get-tuple-element.25), kind=kLoop, calls=%fused_computation.60 | loop fusion | flops 786432 | bytes 2621440 | tf_op jit(solution)/shard_map/convert_element_type | solution.py:41
  28.7 1.1 copy.382
  29.8 4.2 %collective-permute-start.5 = (bf16[2,128,1024]{2,1,0:T(8,128)(2,1)}, bf16[2,128,1024]{2,1,0:T(8,128)(2,1)}, u32[]{:S(2)}, u32[]{:S(2)}) collective-permute-start(bf16[2,128,1024]{2,1,0:T(8,128)(2,1)} %bitcast.138), channel_id=1, source_target_pairs={{0,2},{2,0},{1,3},{3,1},{4,6},{6,4},{5,7},{7,5},{8,10},{10,8},{9,1... | collective-permute-start | bytes 1572872 | tf_op jit(solution)/shard_map/ppermute | solution.py:34
  34.0 9.3 %collective-permute-done = bf16[2,128,1024]{2,1,0:T(8,128)(2,1)} collective-permute-done((bf16[2,128,1024]{2,1,0:T(8,128)(2,1)}, bf16[2,128,1024]{2,1,0:T(8,128)(2,1)}, u32[]{:S(2)}, u32[]{:S(2)}) %collective-permute-start) | collective-permute-done | bytes 524320 | tf_op jit(solution)/shard_map/ppermute | solution.py:18
  43.3 4.1 %collective-permute-done.1 = bf16[2,128,1024]{2,1,0:T(8,128)(2,1)} collective-permute-done((bf16[2,128,1024]{2,1,0:T(8,128)(2,1)}, bf16[2,128,1024]{2,1,0:T(8,128)(2,1)}, u32[]{:S(2)}, u32[]{:S(2)}) %collective-permute-start.1) | collective-permute-done | bytes 524320 | tf_op jit(solution)/shard_map/ppermute | solution.py:20
  47.5 1.4 pad_maximum_fusion.3
  49.2 1.2 fusion.92
  50.4 2.3 %copy.212 = bf16[1,1,384,1024]{2,3,1,0:T(8,128)(2,1)} copy(bf16[1,1,384,1024]{3,2,1,0:T(8,128)(2,1)} %get-tuple-element.18) | data formatting | bytes 1572864 | tf_op jit(solution)/shard_map/slice | solution.py:61
  52.7 1.8 %fusion.99 = (bf16[1,128,1024]{2,1,0:T(8,128)(2,1)S(1)}, bf16[1,128,1024]{2,1,0:T(8,128)(2,1)}) fusion(bf16[2,128,1024]{2,1,0:T(8,128)(2,1)} %copy-done.32), kind=kLoop, calls=%fused_computation.162 | loop fusion | bytes 1048576 | tf_op jit(solution)/shard_map/slice | solution.py:83
  54.4 1.1 copy.216
  55.6 1.2 copy.211
  57.6 1.2 copy.257
  58.7 1.2 copy.256
  61.0 1.7 fusion.116
  63.8 1.4 fusion.110
  65.2 1.2 broadcast_select_fusion.5
  66.7 1.6 copy.225
  69.1 2.3 %fusion.26 = bf16[2,128,1,1024]{3,2,1,0:T(2,128)(2,1)S(1)} fusion(f32[2,128,1,1024]{3,0,2,1:T(2,128)S(1)} %get-tuple-element.24, f32[2,128,1,1024]{3,0,2,1:T(2,128)S(1)} %get-tuple-element.23), kind=kLoop, calls=%fused_computation.61 | loop fusion | flops 786432 | bytes 2621440 | tf_op jit(solution)/shard_map/convert_element_type | solution.py:41
  73.4 1.9 %fusion.98 = (bf16[1,128,1024]{2,1,0:T(8,128)(2,1)}, bf16[1,128,1024]{2,1,0:T(8,128)(2,1)}) fusion(bf16[2,128,1024]{2,1,0:T(8,128)(2,1)} %collective-permute-done.5), kind=kLoop, calls=%fused_computation.161 | loop fusion | bytes 1048576 | tf_op jit(solution)/shard_map/slice | solution.py:83
  75.2 1.8 %copy.222 = bf16[1,128,1024]{1,2,0:T(8,128)(2,1)} copy(bf16[1,128,1024]{2,1,0:T(8,128)(2,1)} %get-tuple-element.42) | data formatting | bytes 524288 | tf_op jit(solution)/shard_map/slice | solution.py:61
  77.0 1.8 %copy.246 = bf16[1,128,1024]{1,2,0:T(8,128)(2,1)} copy(bf16[1,128,1024]{2,1,0:T(8,128)(2,1)} %get-tuple-element.41) | data formatting | bytes 524288 | tf_op jit(solution)/shard_map/slice | solution.py:83
  78.8 2.1 %fusion.115 = (f32[8,128]{1,0:T(8,128)S(1)}, f32[8,128,128]{1,2,0:T(8,128)}) fusion(bf16[128,8,128]{0,2,1:T(8,128)(2,1)} %bitcast.178, bf16[128,8,128]{0,2,1:T(8,128)(2,1)S(1)} %bitcast.142), kind=kOutput, calls=%fused_computation.178 | convolution fusion | flops 33815552 | bytes 1052672 | tf_op jit(solution)/shard_map/gqhd,gkhd->ghqk/dot_general | solution.py:63
  81.0 2.1 %fusion.109 = (f32[8,128]{1,0:T(8,128)S(1)}, f32[8,128,128]{1,2,0:T(8,128)}) fusion(bf16[128,8,128]{0,2,1:T(8,128)(2,1)} %bitcast.179, bf16[128,8,128]{0,2,1:T(8,128)(2,1)} %bitcast.148), kind=kOutput, calls=%fused_computation.172 | convolution fusion | flops 33815552 | bytes 1052672 | tf_op jit(solution)/shard_map/gqhd,gkhd->ghqk/dot_general | solution.py:63
  83.1 14.5 %collective-permute-done.6 = bf16[2,128,1024]{2,1,0:T(8,128)(2,1)} collective-permute-done((bf16[2,128,1024]{2,1,0:T(8,128)(2,1)}, bf16[2,128,1024]{2,1,0:T(8,128)(2,1)}, u32[]{:S(2)}, u32[]{:S(2)}) %collective-permute-start.6) | collective-permute-done | bytes 524320 | tf_op jit(solution)/shard_map/ppermute | solution.py:34
  97.6 1.2 broadcast_select_fusion.3
  99.1 1.6 copy.231
  101.5 2.1 %fusion.27 = bf16[2,128,1,1024]{3,2,1,0:T(2,128)(2,1)S(1)} fusion(f32[2,128,1,1024]{3,0,2,1:T(2,128)S(1)} %get-tuple-element.22, f32[2,128,1,1024]{3,0,2,1:T(2,128)S(1)} %get-tuple-element.21), kind=kLoop, calls=%fused_computation.62 | loop fusion | flops 786432 | bytes 2621440 | tf_op jit(solution)/shard_map/convert_element_type | solution.py:41
  105.6 1.9 %fusion.100 = (bf16[1,128,1024]{2,1,0:T(8,128)(2,1)}, bf16[1,128,1024]{2,1,0:T(8,128)(2,1)}) fusion(bf16[2,128,1024]{2,1,0:T(8,128)(2,1)} %collective-permute-done.6), kind=kLoop, calls=%fused_computation.163 | loop fusion | bytes 1048576 | tf_op jit(solution)/shard_map/slice | solution.py:83
  107.5 1.8 %copy.228 = bf16[1,128,1024]{1,2,0:T(8,128)(2,1)} copy(bf16[1,128,1024]{2,1,0:T(8,128)(2,1)} %get-tuple-element.46) | data formatting | bytes 524288 | tf_op jit(solution)/shard_map/slice | solution.py:61
  109.3 1.8 %copy.248 = bf16[1,128,1024]{1,2,0:T(8,128)(2,1)} copy(bf16[1,128,1024]{2,1,0:T(8,128)(2,1)} %get-tuple-element.45) | data formatting | bytes 524288 | tf_op jit(solution)/shard_map/slice | solution.py:83
  111.1 2.2 %fusion.114 = (f32[8,128]{1,0:T(8,128)S(1)}, f32[8,128,128]{1,2,0:T(8,128)}) fusion(bf16[128,8,128]{0,2,1:T(8,128)(2,1)} %bitcast.180, bf16[128,8,128]{0,2,1:T(8,128)(2,1)S(1)} %bitcast.143), kind=kOutput, calls=%fused_computation.177 | convolution fusion | flops 33815552 | bytes 1052672 | tf_op jit(solution)/shard_map/gqhd,gkhd->ghqk/dot_general | solution.py:63
  113.2 2.1 %fusion.108 = (f32[8,128]{1,0:T(8,128)S(1)}, f32[8,128,128]{1,2,0:T(8,128)}) fusion(bf16[128,8,128]{0,2,1:T(8,128)(2,1)} %bitcast.181, bf16[128,8,128]{0,2,1:T(8,128)(2,1)} %bitcast.149), kind=kOutput, calls=%fused_computation.171 | convolution fusion | flops 33815552 | bytes 1052672 | tf_op jit(solution)/shard_map/gqhd,gkhd->ghqk/dot_general | solution.py:63
  115.3 1.2 broadcast_select_fusion.1
  116.8 1.6 copy.237
  119.2 2.4 %fusion.28 = bf16[2,128,1,1024]{3,2,1,0:T(2,128)(2,1)S(1)} fusion(f32[2,128,1,1024]{3,0,2,1:T(2,128)S(1)} %get-tuple-element.20, f32[2,128,1,1024]{3,0,2,1:T(2,128)S(1)} %get-tuple-element.19), kind=kLoop, calls=%fused_computation.63 | loop fusion | flops 786432 | bytes 2621440 | tf_op jit(solution)/shard_map/convert_element_type | solution.py:41
  122.9 1.9 %fusion.101 = (bf16[1,128,1024]{2,1,0:T(8,128)(2,1)}, bf16[1,128,1024]{2,1,0:T(8,128)(2,1)}) fusion(bf16[2,128,1024]{2,1,0:T(8,128)(2,1)} %collective-permute-done.7), kind=kLoop, calls=%fused_computation.164 | loop fusion | bytes 1048576 | tf_op jit(solution)/shard_map/slice | solution.py:83
  124.8 1.8 %copy.234 = bf16[1,128,1024]{1,2,0:T(8,128)(2,1)} copy(bf16[1,128,1024]{2,1,0:T(8,128)(2,1)} %get-tuple-element.48) | data formatting | bytes 524288 | tf_op jit(solution)/shard_map/slice | solution.py:61
  126.6 1.8 %copy.250 = bf16[1,128,1024]{1,2,0:T(8,128)(2,1)} copy(bf16[1,128,1024]{2,1,0:T(8,128)(2,1)} %get-tuple-element.47) | data formatting | bytes 524288 | tf_op jit(solution)/shard_map/slice | solution.py:83
  128.4 2.0 %fusion.113 = (f32[8,128]{1,0:T(8,128)S(1)}, f32[8,128,128]{1,2,0:T(8,128)}) fusion(bf16[128,8,128]{0,2,1:T(8,128)(2,1)} %bitcast.182, bf16[128,8,128]{0,2,1:T(8,128)(2,1)S(1)} %bitcast.144), kind=kOutput, calls=%fused_computation.176 | convolution fusion | flops 33815552 | bytes 1052672 | tf_op jit(solution)/shard_map/gqhd,gkhd->ghqk/dot_general | solution.py:63
  130.4 2.1 %fusion.107 = (f32[8,128]{1,0:T(8,128)S(1)}, f32[8,128,128]{1,2,0:T(8,128)}) fusion(bf16[128,8,128]{0,2,1:T(8,128)(2,1)} %bitcast.183, bf16[128,8,128]{0,2,1:T(8,128)(2,1)} %bitcast.150), kind=kOutput, calls=%fused_computation.170 | convolution fusion | flops 33815552 | bytes 1052672 | tf_op jit(solution)/shard_map/gqhd,gkhd->ghqk/dot_general | solution.py:63
  132.6 4.6 %collective-permute-done.8 = bf16[2,128,1024]{2,1,0:T(8,128)(2,1)} collective-permute-done((bf16[2,128,1024]{2,1,0:T(8,128)(2,1)}, bf16[2,128,1024]{2,1,0:T(8,128)(2,1)}, u32[]{:S(2)}, u32[]{:S(2)}) %collective-permute-start.8) | collective-permute-done | bytes 524320 | tf_op jit(solution)/shard_map/ppermute | solution.py:34
  137.2 1.9 %fusion.102 = (bf16[1,128,1024]{2,1,0:T(8,128)(2,1)}, bf16[1,128,1024]{2,1,0:T(8,128)(2,1)}) fusion(bf16[2,128,1024]{2,1,0:T(8,128)(2,1)} %collective-permute-done.8), kind=kLoop, calls=%fused_computation.165 | loop fusion | bytes 1048576 | tf_op jit(solution)/shard_map/slice | solution.py:61
  139.1 1.8 %copy.240 = bf16[1,128,1024]{1,2,0:T(8,128)(2,1)} copy(bf16[1,128,1024]{2,1,0:T(8,128)(2,1)} %get-tuple-element.49) | data formatting | bytes 524288 | tf_op jit(solution)/shard_map/slice | solution.py:61
  140.9 1.4 fusion.112
  142.3 2.3 %fusion.106 = (f32[8,128]{1,0:T(8,128)S(1)}, f32[8,128,128]{1,2,0:T(8,128)}) fusion(bf16[128,8,128]{0,2,1:T(8,128)(2,1)} %bitcast.185, bf16[128,8,128]{0,2,1:T(8,128)(2,1)} %bitcast.151), kind=kOutput, calls=%fused_computation.169 | convolution fusion | flops 33815552 | bytes 1052672 | tf_op jit(solution)/shard_map/gqhd,gkhd->ghqk/dot_general | solution.py:63
  145.5 2.4 %fusion.32 = f32[8,128,128]{2,1,0:T(8,128)} fusion(bf16[384,8,128]{0,2,1:T(8,128)(2,1)} %bitcast.165, f32[8,128,384]{1,2,0:T(8,128)S(1)} %get-tuple-element.81, f32[8,128]{1,0:T(8,128)S(1)} %maximum_maximum_fusion.1), kind=kOutput, calls=%fused_computation.66 | convolution fusion | flops 101449728 | bytes 2887680 | tf_op jit(solution)/shard_map/ghqk,gkhd->gqhd/dot_general | solution.py:84
  147.9 2.1 %fusion.71 = f32[8,128,128]{2,1,0:T(8,128)} fusion(bf16[128,8,128]{0,2,1:T(8,128)(2,1)} %bitcast.170, f32[8,128,128]{1,2,0:T(8,128)S(1)} %copy-done.14, f32[8,128]{1,0:T(8,128)S(1)} %maximum_maximum_fusion.1), kind=kOutput, calls=%fused_computation.125 | convolution fusion | flops 33816576 | bytes 1314816 | tf_op jit(solution)/shard_map/ghqk,gkhd->gqhd/dot_general | solution.py:84
  151.1 1.8 %copy.252 = bf16[1,128,1024]{1,2,0:T(8,128)(2,1)} copy(bf16[1,128,1024]{2,1,0:T(8,128)(2,1)} %get-tuple-element.50) | data formatting | bytes 524288 | tf_op jit(solution)/shard_map/slice | solution.py:83
  152.9 1.3 fusion.67
  154.2 1.3 convolution_add_fusion.3
  156.6 2.1 %copy.255 = f32[128,1024]{1,0:T(8,128)} copy(f32[128,1024]{0,1:T(8,128)} %bitcast.191) | data formatting | bytes 1048576 | tf_op jit(solution)/shard_map/add | solution.py:90
  159.0 2.0 %fusion.63 = f32[8,128,128]{2,1,0:T(8,128)} fusion(bf16[128,8,128]{0,2,1:T(8,128)(2,1)} %bitcast.171, f32[8,128,128]{1,2,0:T(8,128)S(1)} %copy-done.12, f32[8,128]{1,0:T(8,128)S(1)} %maximum_maximum_fusion), kind=kOutput, calls=%fused_computation.122 | convolution fusion | flops 33816576 | bytes 1314816 | tf_op jit(solution)/shard_map/ghqk,gkhd->gqhd/dot_general | solution.py:84
  161.1 2.0 %fusion.61 = f32[8,128,128]{2,1,0:T(8,128)} fusion(bf16[128,8,128]{0,2,1:T(8,128)(2,1)} %bitcast.172, f32[8,128,128]{1,2,0:T(8,128)S(1)} %copy-done.15, f32[8,128]{1,0:T(8,128)S(1)} %maximum_maximum_fusion), kind=kOutput, calls=%fused_computation.121 | convolution fusion | flops 33816576 | bytes 1314816 | tf_op jit(solution)/shard_map/ghqk,gkhd->gqhd/dot_general | solution.py:84
  164.7 1.7 fusion.30
  (137 shorter events, 24.0 us)
Async XLA Ops:
  3.8 5.5 %copy-start.38 = (s32[256]{0:T(256)S(1)}, s32[256]{0:T(256)}, u32[]{:S(2)}) copy-start(s32[256]{0:T(256)} %param.7) | copy-start | bytes 3076
  3.9 8.7 %copy-start.7 = (bf16[256,1024]{1,0:T(8,128)(2,1)S(1)}, bf16[256,1024]{1,0:T(8,128)(2,1)}, u32[]{:S(2)}) copy-start(bf16[256,1024]{1,0:T(8,128)(2,1)} %param.6) | copy-start | bytes 1572868
  3.9 8.7 %copy-start.8 = (bf16[256,1024]{1,0:T(8,128)(2,1)S(1)}, bf16[256,1024]{1,0:T(8,128)(2,1)}, u32[]{:S(2)}) copy-start(bf16[256,1024]{1,0:T(8,128)(2,1)} %param.5) | copy-start | bytes 1572868
  6.4 16.8 %collective-permute-start.4 = (bf16[2,128,1024]{2,1,0:T(8,128)(2,1)}, bf16[2,128,1024]{2,1,0:T(8,128)(2,1)S(1)}, u32[]{:S(2)}, u32[]{:S(2)}) collective-permute-start(bf16[2,128,1024]{2,1,0:T(8,128)(2,1)} %bitcast.139), channel_id=1, source_target_pairs={{0,1},{1,0},{2,3},{3,2},{4,5},{5,4},{6,7},{7,6},{8,9},{9,8},{10,11... | collective-permute-start | bytes 1572872 | tf_op jit(solution)/shard_map/ppermute | solution.py:34
  9.4 13.5 %collective-permute-start.2 = (bf16[1,128]{1,0:T(2,128)(2,1)S(1)}, bf16[1,128]{1,0:T(2,128)(2,1)S(1)}, u32[]{:S(2)}, u32[]{:S(2)}) collective-permute-start(bf16[1,128]{1,0:T(2,128)(2,1)S(1)} %get-tuple-element.56), channel_id=1, source_target_pairs={{0,1},{1,2},{2,3},{3,4},{4,5},{5,6},{6,7},{7,8},{8,9},{9,10},{10,1... | collective-permute-start | bytes 776 | tf_op jit(solution)/shard_map/ppermute | solution.py:18
  11.3 11.6 %collective-permute-start.3 = (bf16[1,128]{1,0:T(2,128)(2,1)S(1)}, bf16[1,128]{1,0:T(2,128)(2,1)S(1)}, u32[]{:S(2)}, u32[]{:S(2)}) collective-permute-start(bf16[1,128]{1,0:T(2,128)(2,1)S(1)} %get-tuple-element.57), channel_id=1, source_target_pairs={{1,0},{2,1},{3,2},{4,3},{5,4},{6,5},{7,6},{8,7},{9,8},{10,9},{11,1... | collective-permute-start | bytes 776 | tf_op jit(solution)/shard_map/ppermute | solution.py:20
  13.7 29.7 %collective-permute-start = (bf16[2,128,1024]{2,1,0:T(8,128)(2,1)}, bf16[2,128,1024]{2,1,0:T(8,128)(2,1)}, u32[]{:S(2)}, u32[]{:S(2)}) collective-permute-start(bf16[2,128,1024]{2,1,0:T(8,128)(2,1)} %get-tuple-element.29), channel_id=1, source_target_pairs={{0,1},{1,2},{2,3},{3,4},{4,5},{5,6},{6,7},{7,8},{8,9},{9,10},{10,1... | collective-permute-start | bytes 1572872 | tf_op jit(solution)/shard_map/ppermute | solution.py:18
  20.0 27.4 %collective-permute-start.1 = (bf16[2,128,1024]{2,1,0:T(8,128)(2,1)}, bf16[2,128,1024]{2,1,0:T(8,128)(2,1)}, u32[]{:S(2)}, u32[]{:S(2)}) collective-permute-start(bf16[2,128,1024]{2,1,0:T(8,128)(2,1)} %get-tuple-element.30), channel_id=1, source_target_pairs={{1,0},{2,1},{3,2},{4,3},{5,4},{6,5},{7,6},{8,7},{9,8},{10,9},{11,1... | collective-permute-start | bytes 1572872 | tf_op jit(solution)/shard_map/ppermute | solution.py:20
  22.9 39.8 %copy-start = (bf16[128,1024]{0,1:T(8,128)(2,1)}, bf16[128,1024]{0,1:T(8,128)(2,1)S(1)}, u32[]{:S(2)}) copy-start(bf16[128,1024]{0,1:T(8,128)(2,1)S(1)} %copy.329) | copy-start | bytes 786436
  23.2 0.8 copy-start.32
  28.7 20.1 %copy-start.1 = (bf16[2,128,1,1024]{3,2,1,0:T(2,128)(2,1)}, bf16[2,128,1,1024]{3,2,1,0:T(2,128)(2,1)S(1)}, u32[]{:S(2)}) copy-start(bf16[2,128,1,1024]{3,2,1,0:T(2,128)(2,1)S(1)} %fusion.25) | copy-start | bytes 1572868
  29.8 35.4 %collective-permute-start.5 = (bf16[2,128,1024]{2,1,0:T(8,128)(2,1)}, bf16[2,128,1024]{2,1,0:T(8,128)(2,1)}, u32[]{:S(2)}, u32[]{:S(2)}) collective-permute-start(bf16[2,128,1024]{2,1,0:T(8,128)(2,1)} %bitcast.138), channel_id=1, source_target_pairs={{0,2},{2,0},{1,3},{3,1},{4,6},{6,4},{5,7},{7,5},{8,10},{10,8},{9,1... | collective-permute-start | bytes 1572872 | tf_op jit(solution)/shard_map/ppermute | solution.py:34
  61.0 2.8 %copy-start.25 = (bf16[1,1,384,1024]{2,3,1,0:T(8,128)(2,1)S(1)}, bf16[1,1,384,1024]{2,3,1,0:T(8,128)(2,1)}, u32[]{:S(2)}) copy-start(bf16[1,1,384,1024]{2,3,1,0:T(8,128)(2,1)} %copy.257) | copy-start | bytes 2359300
  62.7 2.5 %copy-start.2 = (bf16[2,128,1,1024]{3,2,1,0:T(2,128)(2,1)S(1)}, bf16[2,128,1,1024]{3,2,1,0:T(2,128)(2,1)}, u32[]{:S(2)}) copy-start(bf16[2,128,1,1024]{3,2,1,0:T(2,128)(2,1)} %copy-done.1) | copy-start | bytes 1572868
  71.4 1.0 copy-start.3
  73.4 24.2 %collective-permute-start.6 = (bf16[2,128,1024]{2,1,0:T(8,128)(2,1)}, bf16[2,128,1024]{2,1,0:T(8,128)(2,1)}, u32[]{:S(2)}, u32[]{:S(2)}) collective-permute-start(bf16[2,128,1024]{2,1,0:T(8,128)(2,1)} %bitcast.137), channel_id=1, source_target_pairs={{0,4},{4,0},{1,5},{5,1},{2,6},{6,2},{3,7},{7,3},{8,12},{12,8},{9,1... | collective-permute-start | bytes 1572872 | tf_op jit(solution)/shard_map/ppermute | solution.py:34
  78.8 18.8 %copy-start.4 = (bf16[2,128,1,1024]{3,2,1,0:T(2,128)(2,1)S(1)}, bf16[2,128,1,1024]{3,2,1,0:T(2,128)(2,1)}, u32[]{:S(2)}) copy-start(bf16[2,128,1,1024]{3,2,1,0:T(2,128)(2,1)} %copy-done.3) | copy-start | bytes 1572868
  103.6 1.0 copy-start.5
  105.5 9.8 %collective-permute-start.7 = (bf16[2,128,1024]{2,1,0:T(8,128)(2,1)}, bf16[2,128,1024]{2,1,0:T(8,128)(2,1)}, u32[]{:S(2)}, u32[]{:S(2)}) collective-permute-start(bf16[2,128,1024]{2,1,0:T(8,128)(2,1)} %bitcast.136), channel_id=1, source_target_pairs={{0,8},{8,0},{1,9},{9,1},{2,10},{10,2},{3,11},{11,3},{4,12},{12,4},... | collective-permute-start | bytes 1572872 | tf_op jit(solution)/shard_map/ppermute | solution.py:34
  111.1 4.3 %copy-start.6 = (bf16[2,128,1,1024]{3,2,1,0:T(2,128)(2,1)S(1)}, bf16[2,128,1,1024]{3,2,1,0:T(2,128)(2,1)}, u32[]{:S(2)}) copy-start(bf16[2,128,1,1024]{3,2,1,0:T(2,128)(2,1)} %copy-done.5) | copy-start | bytes 1572868
  122.5 14.6 %collective-permute-start.8 = (bf16[2,128,1024]{2,1,0:T(8,128)(2,1)}, bf16[2,128,1024]{2,1,0:T(8,128)(2,1)}, u32[]{:S(2)}, u32[]{:S(2)}) collective-permute-start(bf16[2,128,1024]{2,1,0:T(8,128)(2,1)} %bitcast.135), channel_id=1, source_target_pairs={{0,16},{16,0},{1,17},{17,1},{2,18},{18,2},{3,19},{19,3},{4,20},{20... | collective-permute-start | bytes 1572872 | tf_op jit(solution)/shard_map/ppermute | solution.py:34
  140.9 3.9 %copy-start.10 = (f32[8,128,128]{1,2,0:T(8,128)S(1)}, f32[8,128,128]{1,2,0:T(8,128)}, u32[]{:S(2)}) copy-start(f32[8,128,128]{1,2,0:T(8,128)} %get-tuple-element.83) | copy-start | bytes 1572868
  140.9 4.0 %copy-start.13 = (f32[8,128,128]{1,2,0:T(8,128)S(1)}, f32[8,128,128]{1,2,0:T(8,128)}, u32[]{:S(2)}) copy-start(f32[8,128,128]{1,2,0:T(8,128)} %get-tuple-element.77) | copy-start | bytes 1572868
  140.9 4.0 %copy-start.17 = (f32[8,128,128]{1,2,0:T(8,128)S(1)}, f32[8,128,128]{1,2,0:T(8,128)}, u32[]{:S(2)}) copy-start(f32[8,128,128]{1,2,0:T(8,128)} %get-tuple-element.75) | copy-start | bytes 1572868
  140.9 4.0 %copy-start.23 = (f32[8,128,128]{1,2,0:T(8,128)S(1)}, f32[8,128,128]{1,2,0:T(8,128)}, u32[]{:S(2)}) copy-start(f32[8,128,128]{1,2,0:T(8,128)} %get-tuple-element.79) | copy-start | bytes 1572868
  142.3 3.1 %copy-start.19 = (f32[8,128,128]{1,2,0:T(8,128)}, f32[8,128,128]{1,2,0:T(8,128)S(1)}, u32[]{:S(2)}) copy-start(f32[8,128,128]{1,2,0:T(8,128)S(1)} %get-tuple-element.73) | copy-start | bytes 1572868
  145.4 2.5 %copy-start.14 = (f32[8,128,128]{1,2,0:T(8,128)S(1)}, f32[8,128,128]{1,2,0:T(8,128)}, u32[]{:S(2)}) copy-start(f32[8,128,128]{1,2,0:T(8,128)} %get-tuple-element.77) | copy-start | bytes 1572868
  145.4 4.6 %copy-start.18 = (f32[8,128,128]{1,2,0:T(8,128)S(1)}, f32[8,128,128]{1,2,0:T(8,128)}, u32[]{:S(2)}) copy-start(f32[8,128,128]{1,2,0:T(8,128)} %get-tuple-element.75) | copy-start | bytes 1572868
  145.4 4.6 %copy-start.27 = (bf16[1,128,1024]{1,2,0:T(8,128)(2,1)S(1)}, bf16[1,128,1024]{1,2,0:T(8,128)(2,1)}, u32[]{:S(2)}) copy-start(bf16[1,128,1024]{1,2,0:T(8,128)(2,1)} %copy.250) | copy-start | bytes 786436
  147.9 5.0 %copy-start.20 = (f32[8,128,128]{1,2,0:T(8,128)S(1)}, f32[8,128,128]{1,2,0:T(8,128)}, u32[]{:S(2)}) copy-start(f32[8,128,128]{1,2,0:T(8,128)} %copy-done.19) | copy-start | bytes 1572868
  147.9 6.3 %copy-start.11 = (f32[8,128,128]{1,2,0:T(8,128)S(1)}, f32[8,128,128]{1,2,0:T(8,128)}, u32[]{:S(2)}) copy-start(f32[8,128,128]{1,2,0:T(8,128)} %get-tuple-element.83) | copy-start | bytes 1572868
  147.9 6.3 %copy-start.26 = (bf16[1,128,1024]{1,2,0:T(8,128)(2,1)S(1)}, bf16[1,128,1024]{1,2,0:T(8,128)(2,1)}, u32[]{:S(2)}) copy-start(bf16[1,128,1024]{1,2,0:T(8,128)(2,1)} %copy.244) | copy-start | bytes 786436
  151.1 4.5 %copy-start.24 = (f32[8,128,128]{1,2,0:T(8,128)S(1)}, f32[8,128,128]{1,2,0:T(8,128)}, u32[]{:S(2)}) copy-start(f32[8,128,128]{1,2,0:T(8,128)} %get-tuple-element.79) | copy-start | bytes 1572868
  152.9 2.6 %copy-start.29 = (bf16[1,128,1024]{1,2,0:T(8,128)(2,1)S(1)}, bf16[1,128,1024]{1,2,0:T(8,128)(2,1)}, u32[]{:S(2)}) copy-start(bf16[1,128,1024]{1,2,0:T(8,128)(2,1)} %copy.246) | copy-start | bytes 786436
  152.9 2.6 %copy-start.36 = (f32[8,128,128]{2,1,0:T(8,128)S(1)}, f32[8,128,128]{2,1,0:T(8,128)}, u32[]{:S(2)}) copy-start(f32[8,128,128]{2,1,0:T(8,128)} %fusion.71) | copy-start | bytes 1572868
  152.9 2.6 %copy-start.37 = (f32[8,128,128]{2,1,0:T(8,128)S(1)}, f32[8,128,128]{2,1,0:T(8,128)}, u32[]{:S(2)}) copy-start(f32[8,128,128]{2,1,0:T(8,128)} %fusion.69) | copy-start | bytes 1572868
  156.6 2.4 %copy-start.12 = (f32[8,128,128]{1,2,0:T(8,128)S(1)}, f32[8,128,128]{1,2,0:T(8,128)}, u32[]{:S(2)}) copy-start(f32[8,128,128]{1,2,0:T(8,128)} %get-tuple-element.65) | copy-start | bytes 1572868
  156.6 4.5 %copy-start.15 = (f32[8,128,128]{1,2,0:T(8,128)S(1)}, f32[8,128,128]{1,2,0:T(8,128)}, u32[]{:S(2)}) copy-start(f32[8,128,128]{1,2,0:T(8,128)} %get-tuple-element.63) | copy-start | bytes 1572868
  158.7 4.3 %copy-start.16 = (f32[8,128,128]{1,2,0:T(8,128)S(1)}, f32[8,128,128]{1,2,0:T(8,128)}, u32[]{:S(2)}) copy-start(f32[8,128,128]{1,2,0:T(8,128)} %get-tuple-element.61) | copy-start | bytes 1572868
  158.7 4.3 %copy-start.28 = (bf16[1,128,1024]{1,2,0:T(8,128)(2,1)S(1)}, bf16[1,128,1024]{1,2,0:T(8,128)(2,1)}, u32[]{:S(2)}) copy-start(bf16[1,128,1024]{1,2,0:T(8,128)(2,1)} %copy.252) | copy-start | bytes 786436
  159.0 5.1 %copy-start.9 = (f32[8,128,128]{1,2,0:T(8,128)S(1)}, f32[8,128,128]{1,2,0:T(8,128)}, u32[]{:S(2)}) copy-start(f32[8,128,128]{1,2,0:T(8,128)} %get-tuple-element.71) | copy-start | bytes 1572868
  159.0 5.1 %copy-start.21 = (f32[8,128,128]{1,2,0:T(8,128)S(1)}, f32[8,128,128]{1,2,0:T(8,128)}, u32[]{:S(2)}) copy-start(f32[8,128,128]{1,2,0:T(8,128)} %get-tuple-element.67) | copy-start | bytes 1572868
  164.7 2.0 %copy-start.22 = (f32[8,128,128]{1,2,0:T(8,128)S(1)}, f32[8,128,128]{1,2,0:T(8,128)}, u32[]{:S(2)}) copy-start(f32[8,128,128]{1,2,0:T(8,128)} %get-tuple-element.67) | copy-start | bytes 1572868
  164.7 2.0 %copy-start.30 = (bf16[1,128,1024]{1,2,0:T(8,128)(2,1)S(1)}, bf16[1,128,1024]{1,2,0:T(8,128)(2,1)}, u32[]{:S(2)}) copy-start(bf16[1,128,1024]{1,2,0:T(8,128)(2,1)} %copy.246) | copy-start | bytes 786436
  164.7 2.0 %copy-start.33 = (f32[8,128,128]{2,1,0:T(8,128)S(1)}, f32[8,128,128]{2,1,0:T(8,128)}, u32[]{:S(2)}) copy-start(f32[8,128,128]{2,1,0:T(8,128)} %fusion.63) | copy-start | bytes 1572868
  164.7 2.0 %copy-start.34 = (f32[8,128,128]{2,1,0:T(8,128)S(1)}, f32[8,128,128]{2,1,0:T(8,128)}, u32[]{:S(2)}) copy-start(f32[8,128,128]{2,1,0:T(8,128)} %fusion.61) | copy-start | bytes 1572868
  164.7 2.0 %copy-start.35 = (f32[8,128,128]{2,1,0:T(8,128)S(1)}, f32[8,128,128]{2,1,0:T(8,128)}, u32[]{:S(2)}) copy-start(f32[8,128,128]{2,1,0:T(8,128)} %fusion.59) | copy-start | bytes 1572868
  166.7 1.0 copy-start.31
where the time goes:
time: 170 us; the launch traced here: 169 us
  local copies, waits for them, and re-layouts  56.6 us (33%)
  matrix products  38 us (22%)
  waiting for transfers between devices  32.6 us (19%)
  other arithmetic  22.4 us (13%)
  starting transfers between devices  18.4 us (11%)
    dot_general x12, matrix products, attend(): jnp.einsum('gqhd,gkhd->ghqk', grouped, key_heads, preferred_element_type=...  21.6 us
    ppermute x5, waiting for transfers between devices, partner_2(): return lax.ppermute(block, axis, route)  19.2 us
    slice x12, local copies, waits for them, and re-layouts, attend(): stacked[1].reshape(group_count, key_span, head_count, HEAD_DIM)  19.1 us
    dot_general x12, matrix products, attend(): jnp.einsum('ghqk,gkhd->gqhd', weights.astype(jnp.bfloat16), value_heads,...  16.4 us
    slice x8, local copies, waits for them, and re-layouts, attend(): key_heads = stacked[0].reshape(group_count, key_span, head_count, HEAD_DIM)  13.6 us
    convert_element_type x5, other arithmetic, coarsen(): return (0.5 * (paired[:, :, 0] + paired[:, :, 1])).astype(jnp.bfloat16)  10.7 us
    ppermute x2, waiting for transfers between devices, padded_2(): lax.ppermute(tail, axis, [(i, (i + 1) % count) for i in range(ends)])  9.31 us
    ppermute x2, starting transfers between devices, padded_2(): lax.ppermute(tail, axis, [(i, (i + 1) % count) for i in range(ends)])  8.29 us
  transfers between devices with their start and end apart: 9, of which 4 were waited for; matrix products, arithmetic and copies ran while one was open for 33% of the time, Pallas kernels for 0%

commit v1 on v0

v1 whole, which is shorter than its diff:
```python
import functools
import math

import jax
import jax.numpy as jnp
from jax import lax
from jax.experimental import pallas as pl
from jax.experimental.pallas import tpu as pltpu
from jax.sharding import PartitionSpec as P

HEAD_DIM = 128
BLOCK = 128
AXES = ("outer", "inner")
MESH = pl.DeviceIdType.MESH
F32 = jnp.float32
BF16 = jnp.bfloat16
HELPERS = {2: 1, 4: 3}


def pair_means(rows):
    half = rows.shape[0] // 2
    r = lax.broadcasted_iota(jnp.int32, (half, rows.shape[0]), 0)
    c = lax.broadcasted_iota(jnp.int32, (half, rows.shape[0]), 1)
    mix = jnp.where(c // 2 == r, 0.5, 0.0).astype(BF16)
    return jnp.dot(mix, rows, preferred_element_type=F32).astype(BF16)


def kernel(
    levels, inner, q_ref, k_ref, v_ref, mod_ref, out_ref,
    node, far, near, near_mod, bias_own, bias_near, m_ref, l_ref, acc_ref,
    far_send, far_recv, near_send, near_recv,
):
    rows = q_ref.shape[0]
    heads = q_ref.shape[1] // HEAD_DIM
    count = 2**levels
    me = lax.axis_index("outer") * inner + lax.axis_index("inner")
    scale = HEAD_DIM**-0.5 * math.log2(math.e)
    own = (k_ref, v_ref)

    def place(d):
        return (d // inner, d % inner)

    def bit(b):
        return me // 2**b % 2

    def flip(b):
        return me + 2**b * (1 - 2 * bit(b))

    after = (me + 1) % count
    before = (me + count - 1) % count

    @pl.when(me == 0)
    def _():
        near[0] = jnp.zeros(near.shape[1:], BF16)
        near_mod[0] = jnp.full(near_mod.shape[1:], -1, jnp.int32)

    @pl.when(me == count - 1)
    def _():
        near[1] = jnp.zeros(near.shape[1:], BF16)
        near_mod[1] = jnp.full(near_mod.shape[1:], -1, jnp.int32)

    for part in range(2):
        node[0, part] = pair_means(own[part][...])

    barrier = pltpu.get_barrier_semaphore()
    for target in [flip(b) for b in range(levels)] + [after, before]:
        pl.semaphore_signal(barrier, inc=1, device_id=place(target), device_id_type=MESH)
    pl.semaphore_wait(barrier, levels + 2)

    def remote(src, dst, send, recv, target):
        return pltpu.make_async_remote_copy(
            src_ref=src, dst_ref=dst, send_sem=send, recv_sem=recv,
            device_id=place(target), device_id_type=MESH,
        )

    def half_rows(h):
        return pl.ds(pl.multiple_of(bit(h) * (BLOCK // 2), BLOCK // 2), BLOCK // 2)

    def level_copy(b, part):
        sems = (far_send.at[b, part, 0], far_recv.at[b, part, 0])
        if b in HELPERS:
            span = half_rows(HELPERS[b])
            return remote(node.at[b, part, span], far.at[b, part, span], *sems, flip(b))
        return remote(node.at[b, part], far.at[b, part], *sems, flip(b))

    def share_copy(b, part):
        span = half_rows(HELPERS[b])
        view = far.at[b, part, span]
        return remote(view, view, far_send.at[b, part, 1], far_recv.at[b, part, 1], flip(HELPERS[b]))

    def near_copies(side):
        target = after if side == 0 else before
        start = rows - BLOCK if side == 0 else 0
        copies = [
            remote(own[part].at[pl.ds(start, BLOCK)], near.at[side, part],
                   near_send.at[side, part], near_recv.at[side, part], target)
            for part in range(2)
        ]
        copies.append(
            remote(mod_ref.at[start // BLOCK], near_mod.at[side],
                   near_send.at[side, 2], near_recv.at[side, 2], target)
        )
        return copies

    def start_near(side):
        for copy in near_copies(side):
            copy.start()

    for part in range(2):
        level_copy(0, part).start()
    pl.when(bit(0) == 0)(lambda: start_near(0))
    pl.when(bit(0) == 1)(lambda: start_near(1))

    def label_rows(i):
        return jnp.broadcast_to(mod_ref[i].astype(F32), (BLOCK, BLOCK))

    labels = [label_rows(0), label_rows(1)]
    columns = [jnp.transpose(x) for x in labels]
    zero = jnp.zeros((BLOCK, BLOCK), F32)
    for i in range(2):
        for j in range(2):
            value = zero if i == j else jnp.where(labels[j] == columns[i], 0.0, -jnp.inf)
            bias_own[i * BLOCK : (i + 1) * BLOCK, j * BLOCK : (j + 1) * BLOCK] = value

    def head_cols(h):
        return pl.ds(pl.multiple_of(h * HEAD_DIM, HEAD_DIM), HEAD_DIM)

    def score(q, k):
        return lax.dot_general(q, k, (((1,), (1,)), ((), ())), preferred_element_type=F32) * scale

    def first(h):
        cols = head_cols(h)
        s = score(q_ref[:, cols], k_ref[:, cols]) + bias_own[...]
        m = jnp.broadcast_to(jnp.max(s, axis=1, keepdims=True), (rows, BLOCK))
        p0 = jnp.exp2(s[:, :BLOCK] - m)
        p1 = jnp.exp2(s[:, BLOCK:] - m)
        m_ref[h] = m
        l_ref[h] = p0 + p1
        p = jnp.concatenate([p0.astype(BF16), p1.astype(BF16)], axis=1)
        acc_ref[h] = jnp.dot(p, v_ref[:, cols], preferred_element_type=F32)

    def merged(h, span, k, v, bias):
        cols = head_cols(h)
        s = score(q_ref[span, cols], k[:, cols])
        if bias is not None:
            s = s + bias[...]
        m_old = m_ref[h, span]
        m = jnp.maximum(m_old, jnp.max(s, axis=1, keepdims=True))
        p = jnp.exp2(s - m)
        a = jnp.exp2(m_old - m)
        l = l_ref[h, span] * a + p
        acc = acc_ref[h, span] * a + jnp.dot(p.astype(BF16), v[:, cols], preferred_element_type=F32)
        return m, l, acc

    def update(h, span, k, v, bias=None):
        m, l, acc = merged(h, span, k, v, bias)
        m_ref[h, span] = m
        l_ref[h, span] = l
        acc_ref[h, span] = acc

    def every_head(body):
        def step(h, carry):
            body(h)
            return carry

        lax.fori_loop(0, heads, step, 0, unroll=2)

    everything = pl.ds(0, rows)

    def near_update(side):
        i = side
        other = jnp.broadcast_to(near_mod[side].astype(F32), (BLOCK, BLOCK))
        mine = jnp.transpose(label_rows(i))
        bias_near[side] = jnp.where(other == mine, 0.0, -jnp.inf)
        every_head(
            lambda h: update(h, pl.ds(i * BLOCK, BLOCK), near.at[side, 0], near.at[side, 1], bias_near.at[side])
        )

    def wait_near(side):
        has = me > 0 if side == 0 else me < count - 1

        @pl.when(has)
        def _():
            for copy in near_copies(side):
                copy.wait_recv()

    def far_head(b):
        def body(h):
            update(h, everything, far.at[b, 0], far.at[b, 1])

        return body

    def last_head(h):
        m, l, acc = merged(h, everything, far.at[levels - 1, 0], far.at[levels - 1, 1], None)
        total = jnp.sum(l, axis=1, keepdims=True)
        out_ref[:, head_cols(h)] = (acc / total).astype(BF16)

    every_head(first)
    for b in range(levels):
        if b in HELPERS:
            for part in range(2):
                level_copy(b, part).wait_recv()
                share_copy(b, part).start()
        if b == levels - 1:
            for side in range(2):
                wait_near(side)
                near_update(side)
        for part in range(2):
            if b in HELPERS:
                share_copy(b, part).wait_recv()
            else:
                level_copy(b, part).wait_recv()
            if b + 1 < levels:
                for source, upper in ((node, bit(b)), (far, 1 - bit(b))):
                    span = pl.ds(pl.multiple_of(upper * (BLOCK // 2), BLOCK // 2), BLOCK // 2)
                    node[b + 1, part, span, :] = pair_means(source[b, part])
                level_copy(b + 1, part).start()
        if b == 0:
            pl.when((bit(0) == 0) & (me > 0))(lambda: start_near(1))
            pl.when((bit(0) == 1) & (me < count - 1))(lambda: start_near(0))
        if b < levels - 1:
            every_head(far_head(b))
    every_head(last_head)

    for b in range(levels):
        for part in range(2):
            level_copy(b, part).wait_send()
            if b in HELPERS:
                share_copy(b, part).wait_send()
    for side, has in ((0, me < count - 1), (1, me > 0)):

        @pl.when(has)
        def _(side=side):
            for copy in near_copies(side):
                copy.wait_send()


def shards(levels, inner, queries, keys, values, modality):
    rows, width = queries.shape
    heads = width // HEAD_DIM
    labels = modality.reshape(rows // BLOCK, 1, BLOCK)
    vmem = pl.BlockSpec(memory_space=pltpu.VMEM)
    state = pltpu.VMEM((heads, rows, HEAD_DIM), F32)
    return pl.pallas_call(
        functools.partial(kernel, levels, inner),
        out_shape=jax.ShapeDtypeStruct((rows, width), BF16),
        in_specs=[vmem] * 4,
        out_specs=vmem,
        scratch_shapes=[
            pltpu.VMEM((levels, 2, BLOCK, width), BF16),
            pltpu.VMEM((levels, 2, BLOCK, width), BF16),
            pltpu.VMEM((2, 2, BLOCK, width), BF16),
            pltpu.VMEM((2, 1, BLOCK), jnp.int32),
            pltpu.VMEM((rows, 2 * BLOCK), F32),
            pltpu.VMEM((2, BLOCK, BLOCK), F32),
            state,
            state,
            state,
            pltpu.SemaphoreType.DMA((levels, 2, 2)),
            pltpu.SemaphoreType.DMA((levels, 2, 2)),
            pltpu.SemaphoreType.DMA((2, 3)),
            pltpu.SemaphoreType.DMA((2, 3)),
        ],
        compiler_params=pltpu.CompilerParams(
            collective_id=0, has_side_effects=True, vmem_limit_bytes=56 * 2**20
        ),
    )(queries, keys, values, labels)


def solution(mesh):
    outer, inner = mesh.shape["outer"], mesh.shape["inner"]
    levels = (outer * inner).bit_length() - 1
    rows = P(AXES, None)
    return jax.shard_map(
        functools.partial(shards, levels, inner),
        mesh=mesh,
        in_specs=(rows, rows, rows, P(AXES)),
        out_specs=rows,
        check_vma=False,
    )
```

time: 170 us -> 70.3 us (0.41)
  the two profiles are of different devices: /device:TPU:0 before, /device:TPU:10 now
where the time goes in v1:
time: 70.3 us; the launch traced here: 70.1 us
  Pallas kernels  68.3 us (97%)
  local copies, waits for them, and re-layouts  1.87 us (3%)
    pallas_call x1, Pallas kernels, shards(): pl.pallas_call(functools.partial(kernel, levels, inner), out_shape=jax.Sh...  68.3 us
    unnamed x1, local copies, waits for them, and re-layouts  1.87 us

profile of v1, /device:TPU:10, one launch (start us, length us, event | category | flops | bytes accessed | tf_op | source)
XLA Modules:
  0.0 70.1 jit_solution(16966291337759271630)
XLA Ops:
  0.0 68.3 %shard_map.46 = bf16[256,1024]{1,0:T(8,128)(2,1)} custom-call(bf16[256,1024]{1,0:T(8,128)(2,1)} %q_ref.1, bf16[256,1024]{1,0:T(8,128)(2,1)} %k_ref.1, bf16[256,1024]{1,0:T(8,128)(2,1)} %v_ref.1, s32[2,1,128]{2,1,0:T(1,128)} %bitcast.1), custom_call_target="tpu_custom_call" | custom-call | tf_op jit(solution)/shard_map/pallas_call | solution.py:244
  68.3 1.9 %copy.6 = bf16[256,1024]{1,0:T(8,128)(2,1)} copy(bf16[256,1024]{1,0:T(8,128)(2,1)} %shard_map.46) | data formatting | bytes 1048576

commit v2 on v1

--- a/solution.py
+++ b/solution.py
@@ -14,7 +14,8 @@
 MESH = pl.DeviceIdType.MESH
 F32 = jnp.float32
 BF16 = jnp.bfloat16
-HELPERS = {2: 1, 4: 3}
+SHARED = (2, 4)
+SPLIT = 1
 
 
 def pair_means(rows):
@@ -73,20 +74,55 @@
             device_id=place(target), device_id_type=MESH,
         )
 
-    def half_rows(h):
-        return pl.ds(pl.multiple_of(bit(h) * (BLOCK // 2), BLOCK // 2), BLOCK // 2)
-
-    def level_copy(b, part):
-        sems = (far_send.at[b, part, 0], far_recv.at[b, part, 0])
-        if b in HELPERS:
-            span = half_rows(HELPERS[b])
-            return remote(node.at[b, part, span], far.at[b, part, span], *sems, flip(b))
-        return remote(node.at[b, part], far.at[b, part], *sems, flip(b))
+    def half_rows(upper):
+        return pl.ds(pl.multiple_of(upper * (BLOCK // 2), BLOCK // 2), BLOCK // 2)
+
+    def whole_copy(b, part):
+        return remote(node.at[b, part], far.at[b, part], far_send.at[b, part, 0], far_recv.at[b, part, 0], flip(b))
+
+    def half_copy(b, part, slot):
+        span = half_rows(bit(b - 1) if slot == 0 else 1 - bit(b - 1))
+        return remote(node.at[b, part, span], far.at[b, part, span],
+                      far_send.at[b, part, slot], far_recv.at[b, part, slot], flip(b))
 
     def share_copy(b, part):
-        span = half_rows(HELPERS[b])
-        view = far.at[b, part, span]
-        return remote(view, view, far_send.at[b, part, 1], far_recv.at[b, part, 1], flip(HELPERS[b]))
+        view = far.at[b, part, half_rows(bit(b - 1))]
+        return remote(view, view, far_send.at[b, part, 1], far_recv.at[b, part, 1], flip(b - 1))
+
+    def level_copies(b, part):
+        if b in SHARED:
+            return [half_copy(b, part, 0), share_copy(b, part)]
+        if b == SPLIT:
+            return [half_copy(b, part, 0), half_copy(b, part, 1)]
+        return [whole_copy(b, part)]
+
+    def own_ready(b, part):
+        if b < levels:
+            node[b, part, half_rows(bit(b - 1)), :] = pair_means(node[b - 1, part])
+            if b in SHARED or b == SPLIT:
+                half_copy(b, part, 0).start()
+
+    def far_ready(b, part):
+        if b < levels:
+            if b not in SHARED or b + 1 < levels:
+                node[b, part, half_rows(1 - bit(b - 1)), :] = pair_means(far[b - 1, part])
+            if b == SPLIT:
+                half_copy(b, part, 1).start()
+            elif b not in SHARED:
+                whole_copy(b, part).start()
+            own_ready(b + 1, part)
+
+    def wait_first(b):
+        if b in SHARED:
+            for part in range(2):
+                half_copy(b, part, 0).wait_recv()
+                share_copy(b, part).start()
+
+    def wait_level(b):
+        for part in range(2):
+            for copy in level_copies(b, part)[1 if b in SHARED else 0 :]:
+                copy.wait_recv()
+            far_ready(b + 1, part)
 
     def near_copies(side):
         target = after if side == 0 else before
@@ -107,7 +143,9 @@
             copy.start()
 
     for part in range(2):
-        level_copy(0, part).start()
+        whole_copy(0, part).start()
+    for part in range(2):
+        own_ready(1, part)
     pl.when(bit(0) == 0)(lambda: start_near(0))
     pl.when(bit(0) == 1)(lambda: start_near(1))
 
@@ -163,26 +201,28 @@
             body(h)
             return carry
 
-        lax.fori_loop(0, heads, step, 0, unroll=2)
+        lax.fori_loop(0, heads, step, 0, unroll=8)
 
     everything = pl.ds(0, rows)
 
     def near_update(side):
         i = side
+        block = pl.ds(pl.multiple_of(side * BLOCK, BLOCK), BLOCK)
         other = jnp.broadcast_to(near_mod[side].astype(F32), (BLOCK, BLOCK))
         mine = jnp.transpose(label_rows(i))
         bias_near[side] = jnp.where(other == mine, 0.0, -jnp.inf)
         every_head(
-            lambda h: update(h, pl.ds(i * BLOCK, BLOCK), near.at[side, 0], near.at[side, 1], bias_near.at[side])
+            lambda h: update(h, block, near.at[side, 0], near.at[side, 1], bias_near.at[side])
         )
 
-    def wait_near(side):
-        has = me > 0 if side == 0 else me < count - 1
-
-        @pl.when(has)
-        def _():
-            for copy in near_copies(side):
-                copy.wait_recv()
+    def wait_pair(turn):
+        for side in range(2):
+            has = me > 0 if side == 0 else me < count - 1
+
+            @pl.when(has & (bit(0) == (1 - side if turn == 0 else side)))
+            def _():
+                for copy in near_copies(side):
+                    copy.wait_recv()
 
     def far_head(b):
         def body(h):
@@ -197,36 +237,25 @@
 
     every_head(first)
     for b in range(levels):
-        if b in HELPERS:
-            for part in range(2):
-                level_copy(b, part).wait_recv()
-                share_copy(b, part).start()
+        wait_first(b)
         if b == levels - 1:
-            for side in range(2):
-                wait_near(side)
-                near_update(side)
-        for part in range(2):
-            if b in HELPERS:
-                share_copy(b, part).wait_recv()
-            else:
-                level_copy(b, part).wait_recv()
-            if b + 1 < levels:
-                for source, upper in ((node, bit(b)), (far, 1 - bit(b))):
-                    span = pl.ds(pl.multiple_of(upper * (BLOCK // 2), BLOCK // 2), BLOCK // 2)
-                    node[b + 1, part, span, :] = pair_means(source[b, part])
-                level_copy(b + 1, part).start()
+            wait_pair(1)
+            near_update(bit(0))
+        wait_level(b)
         if b == 0:
             pl.when((bit(0) == 0) & (me > 0))(lambda: start_near(1))
             pl.when((bit(0) == 1) & (me < count - 1))(lambda: start_near(0))
+        if b == 2:
+            wait_pair(0)
+            near_update(1 - bit(0))
         if b < levels - 1:
             every_head(far_head(b))
     every_head(last_head)
 
     for b in range(levels):
         for part in range(2):
-            level_copy(b, part).wait_send()
-            if b in HELPERS:
-                share_copy(b, part).wait_send()
+            for copy in level_copies(b, part):
+                copy.wait_send()
     for side, has in ((0, me < count - 1), (1, me > 0)):
 
         @pl.when(has)

time: 70.3 us -> 54.9 us (0.78)
  the two profiles are of different devices: /device:TPU:10 before, /device:TPU:0 now
where the time goes in v2:
time: 54.9 us; the launch traced here: 54.7 us
  Pallas kernels  52.8 us (96%)
  local copies, waits for them, and re-layouts  1.87 us (3%)
    pallas_call x1, Pallas kernels, shards(): pl.pallas_call(functools.partial(kernel, levels, inner), out_shape=jax.Sh...  52.8 us
    unnamed x1, local copies, waits for them, and re-layouts  1.87 us

profile of v2, /device:TPU:0, one launch (start us, length us, event | category | flops | bytes accessed | tf_op | source)
XLA Modules:
  0.0 54.7 jit_solution(6766053634811895215)
XLA Ops:
  0.0 52.8 %shard_map.46 = bf16[256,1024]{1,0:T(8,128)(2,1)} custom-call(bf16[256,1024]{1,0:T(8,128)(2,1)} %q_ref.1, bf16[256,1024]{1,0:T(8,128)(2,1)} %k_ref.1, bf16[256,1024]{1,0:T(8,128)(2,1)} %v_ref.1, s32[2,1,128]{2,1,0:T(1,128)} %bitcast.1), custom_call_target="tpu_custom_call" | custom-call | tf_op jit(solution)/shard_map/pallas_call | solution.py:273
  52.9 1.9 %copy.6 = bf16[256,1024]{1,0:T(8,128)(2,1)} copy(bf16[256,1024]{1,0:T(8,128)(2,1)} %shard_map.46) | data formatting | bytes 1048576

commit v3 on v2

--- a/solution.py
+++ b/solution.py
@@ -29,7 +29,7 @@
 def kernel(
     levels, inner, q_ref, k_ref, v_ref, mod_ref, out_ref,
     node, far, near, near_mod, bias_own, bias_near, m_ref, l_ref, acc_ref,
-    far_send, far_recv, near_send, near_recv,
+    far_send, far_recv, near_send, near_recv, relay, relay_send, relay_recv,
 ):
     rows = q_ref.shape[0]
     heads = q_ref.shape[1] // HEAD_DIM
@@ -49,6 +49,8 @@
 
     after = (me + 1) % count
     before = (me + count - 1) % count
+    two_after = (me + 2) % count
+    two_before = (me + count - 2) % count
 
     @pl.when(me == 0)
     def _():
@@ -64,9 +66,9 @@
         node[0, part] = pair_means(own[part][...])
 
     barrier = pltpu.get_barrier_semaphore()
-    for target in [flip(b) for b in range(levels)] + [after, before]:
+    for target in [flip(b) for b in range(levels)] + [after, before, two_after, two_before]:
         pl.semaphore_signal(barrier, inc=1, device_id=place(target), device_id_type=MESH)
-    pl.semaphore_wait(barrier, levels + 2)
+    pl.semaphore_wait(barrier, levels + 4)
 
     def remote(src, dst, send, recv, target):
         return pltpu.make_async_remote_copy(
@@ -142,10 +144,32 @@
         for copy in near_copies(side):
             copy.start()
 
+    def relay_in(side):
+        start = rows - BLOCK if side == 0 else 0
+        return remote(v_ref.at[pl.ds(start, BLOCK)], relay, near_send.at[side, 1], relay_recv,
+                      two_after if side == 0 else two_before)
+
+    def start_cross(side):
+        near_copies(side)[0].start()
+        near_copies(side)[2].start()
+
+    def relay_out(side):
+        return remote(relay, near.at[side, 1], relay_send, near_recv.at[side, 1], flip(0))
+
+    def on_relay(action):
+        pl.when((bit(0) == 0) & (me + 2 < count))(lambda: action(1))
+        pl.when((bit(0) == 1) & (me > 2))(lambda: action(0))
+
+    def hand_over(side):
+        relay_in(side).wait_recv()
+        relay_out(side).start()
+
     for part in range(2):
         whole_copy(0, part).start()
     for part in range(2):
         own_ready(1, part)
+    pl.when((bit(0) == 0) & (me > 0))(lambda: relay_in(1).start())
+    pl.when((bit(0) == 1) & (me < count - 1))(lambda: relay_in(0).start())
     pl.when(bit(0) == 0)(lambda: start_near(0))
     pl.when(bit(0) == 1)(lambda: start_near(1))
 
@@ -238,13 +262,15 @@
     every_head(first)
     for b in range(levels):
         wait_first(b)
+        if b == 1:
+            on_relay(hand_over)
         if b == levels - 1:
             wait_pair(1)
             near_update(bit(0))
         wait_level(b)
         if b == 0:
-            pl.when((bit(0) == 0) & (me > 0))(lambda: start_near(1))
-            pl.when((bit(0) == 1) & (me < count - 1))(lambda: start_near(0))
+            pl.when((bit(0) == 0) & (me > 0))(lambda: start_cross(1))
+            pl.when((bit(0) == 1) & (me < count - 1))(lambda: start_cross(0))
         if b == 2:
             wait_pair(0)
             near_update(1 - bit(0))
@@ -252,6 +278,7 @@
             every_head(far_head(b))
     every_head(last_head)
 
+    on_relay(lambda side: relay_out(side).wait_send())
     for b in range(levels):
         for part in range(2):
             for copy in level_copies(b, part):
@@ -289,6 +316,9 @@
             pltpu.SemaphoreType.DMA((levels, 2, 2)),
             pltpu.SemaphoreType.DMA((2, 3)),
             pltpu.SemaphoreType.DMA((2, 3)),
+            pltpu.VMEM((BLOCK, width), BF16),
+            pltpu.SemaphoreType.DMA(()),
+            pltpu.SemaphoreType.DMA(()),
         ],
         compiler_params=pltpu.CompilerParams(
             collective_id=0, has_side_effects=True, vmem_limit_bytes=56 * 2**20

time: 54.9 us -> 53.8 us (0.980)
  Pallas kernels: 52.8 us -> 51.8 us
    pallas_call x1, Pallas kernels: 52.8 us -> 51.8 us  [shards(): pl.pallas_call(functools.partial(kernel, levels, inner), out_shape=jax.Sh...]
where the time goes in v3:
time: 53.8 us; the launch traced here: 53.6 us
  Pallas kernels  51.8 us (96%)
  local copies, waits for them, and re-layouts  1.87 us (3%)
    pallas_call x1, Pallas kernels, shards(): pl.pallas_call(functools.partial(kernel, levels, inner), out_shape=jax.Sh...  51.8 us
    unnamed x1, local copies, waits for them, and re-layouts  1.87 us

profile of v3, /device:TPU:0, one launch (start us, length us, event | category | flops | bytes accessed | tf_op | source)
XLA Modules:
  0.0 53.6 jit_solution(2627271225604022175)
XLA Ops:
  0.0 51.8 %shard_map.46 = bf16[256,1024]{1,0:T(8,128)(2,1)} custom-call(bf16[256,1024]{1,0:T(8,128)(2,1)} %q_ref.1, bf16[256,1024]{1,0:T(8,128)(2,1)} %k_ref.1, bf16[256,1024]{1,0:T(8,128)(2,1)} %v_ref.1, s32[2,1,128]{2,1,0:T(1,128)} %bitcast.1), custom_call_target="tpu_custom_call" | custom-call | tf_op jit(solution)/shard_map/pallas_call | solution.py:300
  51.8 1.9 %copy.6 = bf16[256,1024]{1,0:T(8,128)(2,1)} copy(bf16[256,1024]{1,0:T(8,128)(2,1)} %shard_map.46) | data formatting | bytes 1048576
